TPU v7x, 256 devices: a whole 4x4x8 slice. The times are simulated.
256 devices in a mesh: wide: 64 (over y, z, core), narrow: 4 (over x).
Axes of the slice: x: 4, y: 4, z: 8, core: 2. Of those that a mesh axis runs over, the one named last changes fastest.
Arguments:
- patches: bfloat16 [65536, 1280], P('wide', 'narrow'), may hold values from -6 to 6
- norm_gain: float32 [1280], replicated, may hold values from 0.1 to 1.9
- norm_bias: float32 [1280], replicated, may hold values from -3 to 3
- w_in: bfloat16 [1280, 5120], P('wide', 'narrow'), may hold values from -0.15625 to 0.15625
- b_in: float32 [5120], P('narrow'), may hold values from -3 to 3
- w_out: bfloat16 [5120, 1280], P('narrow', 'wide'), may hold values from -0.078125 to 0.078125
- b_out: float32 [1280], P('narrow'), may hold values from -3 to 3
- w_proj: bfloat16 [4, 1280, 1280], P(None, 'narrow', 'wide'), may hold values from -0.078125 to 0.078125
- b_proj: float32 [1280], P('narrow'), may hold values from -3 to 3
- text: bfloat16 [32768, 1280], P('wide', 'narrow'), may hold values from -6 to 6
- place: int32 [16384], replicated, may hold values from -1 to 32767, as said below
Outputs:
- prompt_embeds: bfloat16 [32768, 1280], P('wide', 'narrow')
Inputs may be any that keep to these rules, and one draw needn't show every extreme that they name: `place`: of the 256 entries of one wide index (entries i * 256 to (i + 1) * 256 - 1), the valid ones (>= 0) come first and -1 fills the rest; three quarters or more are valid, and all are valid for some wide index. Valid values are distinct. For one wide index, at most 8 valid entries v have the same v // 512, and every wide index reaches 8 for some value.
All inputs are finite; a program needn't handle non-finite values.
Results may differ from a plain program's by a relative error of at most 0.012.
Values may be sent and summed in bfloat16 or wider, within the bound.
A program may use at most 64 MiB of HBM per device.

v0:
```python
import jax
import jax.numpy as jnp
from jax import lax
from jax.sharding import PartitionSpec as P


def per_device(
    patches, norm_gain, norm_bias, w_in, b_in, w_out, b_out, w_proj, b_proj, text, place
):
    whole = lax.all_gather(patches, "narrow", axis=1, tiled=True)
    values = whole.astype(jnp.float32)
    center = jnp.mean(values, axis=-1, keepdims=True)
    spread = jnp.mean(jnp.square(values - center), axis=-1, keepdims=True)
    normed = ((values - center) * lax.rsqrt(spread + 1e-06) * norm_gain + norm_bias).astype(
        jnp.bfloat16
    )
    rows_in, cols_out, proj_cols = (
        lax.all_gather(w_in, "wide", axis=0, tiled=True),
        lax.all_gather(w_out, "wide", axis=1, tiled=True),
        lax.all_gather(w_proj, "wide", axis=2, tiled=True),
    )
    product = jnp.dot(normed, rows_in, preferred_element_type=jnp.float32)
    hidden = jax.nn.gelu(product + b_in, approximate=False).astype(jnp.bfloat16)
    partial_out = jnp.dot(hidden, cols_out, preferred_element_type=jnp.float32)
    mlp_out = lax.psum_scatter(
        partial_out.astype(jnp.bfloat16), "narrow", scatter_dimension=1, tiled=True
    ).astype(jnp.float32)
    stream = (patches.astype(jnp.float32) + (mlp_out + b_out)).astype(jnp.bfloat16)
    merge_count = stream.shape[0] // 4
    merged = stream.reshape(merge_count, 4 * stream.shape[1])
    groups = lax.axis_size("wide")
    own_index = lax.axis_index("wide")
    seq_rows = text.shape[0]
    bucket = seq_rows // groups
    place_table = place.reshape(groups, merge_count)
    owners = jnp.where(place_table >= 0, place_table // seq_rows, groups)
    own_owners = lax.dynamic_index_in_dim(owners, own_index, 0, keepdims=False)
    owner_hits = (own_owners[:, None] == jnp.arange(groups, dtype=jnp.int32)[None, :]).astype(
        jnp.int32
    )
    slot_out = jnp.sum(jnp.cumsum(owner_hits, axis=0) * owner_hits, axis=1) - 1
    slot_out = jnp.where(own_owners < groups, slot_out, bucket)
    arriving = owners == own_index
    slot_in = jnp.cumsum(arriving.astype(jnp.int32), axis=1) - 1
    slot_in = jnp.where(arriving, slot_in, bucket)
    local_row = jnp.where(arriving, place_table % seq_rows, seq_rows)
    source_ids = jnp.arange(groups, dtype=jnp.int32)[:, None]
    targets = (
        jnp.full((groups, bucket), seq_rows, jnp.int32)
        .at[source_ids, slot_in]
        .set(local_row, mode="drop")
    )
    partial_proj = jnp.dot(
        merged, proj_cols.reshape(-1, proj_cols.shape[2]), preferred_element_type=jnp.float32
    )
    vision = (
        lax.psum_scatter(
            partial_proj.astype(jnp.bfloat16), "narrow", scatter_dimension=1, tiled=True
        ).astype(jnp.float32)
        + b_proj
    ).astype(jnp.bfloat16)
    buffer = jnp.zeros((groups, bucket, vision.shape[1]), vision.dtype)
    received = lax.all_to_all(
        buffer.at[own_owners, slot_out].set(vision, mode="drop"),
        "wide",
        split_axis=0,
        concat_axis=0,
        tiled=True,
    )
    return text.at[targets.reshape(-1)].set(received.reshape(-1, received.shape[2]), mode="drop")


def solution(mesh):
    placed = (
        P("wide", "narrow"),
        P(),
        P(),
        P("wide", "narrow"),
        P("narrow"),
        P("narrow", "wide"),
        P("narrow"),
        P(None, "narrow", "wide"),
        P("narrow"),
        P("wide", "narrow"),
        P(),
    )
    return jax.shard_map(
        per_device, mesh=mesh, in_specs=placed, out_specs=P("wide", "narrow"), check_vma=False
    )
```

profile of v0, /device:TPU:1, one launch (start us, length us, event | category | flops | bytes accessed | tf_op | source)
XLA Modules:
  0.0 475.5 jit_solution(18074952579770676036)
XLA Ops:
  6.5 0.7 all-gather.7.cloned.1.call-update
  7.3 0.7 all-gather.13.cloned.1.call-update
  8.1 0.7 all-gather.11.cloned.1.call-update
  8.8 0.5 all-gather.9.cloned.1.call-update
  9.4 41.4 %all-gather.7.cloned.1.call-done = bf16[1024,1280]{0,1:T(8,128)(2,1)} async-done(((bf16[1024,320]{0,1:T(8,128)(2,1)}), bf16[1024,1280]{0,1:T(8,128)(2,1)}) %all-gather.7.cloned.1.call-update) | async-done | bytes 2621456 | tf_op jit(solution)/shard_map/all_gather | solution.py:10
  50.7 2.3 convert_reduce_fusion
  53.2 0.7 fusion.2
  54.0 78.9 %all-gather.13.cloned.1.call-done = bf16[64,20,1280]{2,1,0:T(8,128)(2,1)} async-done(((bf16[1,20,1280]{2,1,0:T(8,128)(2,1)}), bf16[64,20,1280]{2,1,0:T(8,128)(2,1)}) %all-gather.13.cloned.1.call-update) | async-done | bytes 3276816 | tf_op jit(solution)/shard_map/all_gather | solution.py:19
  132.9 6.1 %reshape.317 = bf16[1280,1280]{1,0:T(8,128)(2,1)} reshape(bf16[64,20,1280]{2,1,0:T(8,128)(2,1)} %all-gather.13.cloned.1.call-done) | data formatting | bytes 6553600
  139.1 72.6 %all-gather.11.cloned.1.call-done = bf16[64,20,1280]{2,1,0:T(8,128)(2,1)} async-done(((bf16[1,20,1280]{2,1,0:T(8,128)(2,1)}), bf16[64,20,1280]{2,1,0:T(8,128)(2,1)}) %all-gather.11.cloned.1.call-update) | async-done | bytes 3276816 | tf_op jit(solution)/shard_map/all_gather | solution.py:18
  211.7 6.1 %reshape.315 = bf16[1280,1280]{1,0:T(8,128)(2,1)} reshape(bf16[64,20,1280]{2,1,0:T(8,128)(2,1)} %all-gather.11.cloned.1.call-done) | data formatting | bytes 6553600
  217.8 21.4 %convolution_convert_fusion = bf16[1024,1280]{0,1:T(8,128)(2,1)} fusion(bf16[1280,1280]{1,0:T(8,128)(2,1)} %reshape.317, bf16[1280,1280]{1,0:T(8,128)(2,1)} %reshape.315, bf16[1024,1280]{0,1:T(8,128)(2,1)S(1)} %copy-done, f32[1280]{0:T(1024)S(1)} %copy-done.6, f32[1280]{0:T(1024)S(1)} %copy-done.7, f32[1280]{0:T(1024)S(1)} %copy-done.8, ...), kind=kOutput, calls=%fused_computation.30 | convolution fusion | flops 6806568960 | bytes 11820032 | tf_op jit(solution)/shard_map/dot_general | solution.py:24
  239.4 0.6 reduce-window.14
  240.0 0.2 slice_reduce_fusion.1
  240.4 49.9 %all-gather.9.cloned.1.call-done = bf16[4,320,1280]{1,0,2:T(4,128)(2,1)} async-done(((bf16[4,320,20]{1,0,2:T(4,128)(2,1)}), bf16[4,320,1280]{1,0,2:T(4,128)(2,1)}) %all-gather.9.cloned.1.call-update) | async-done | bytes 3276816 | tf_op jit(solution)/shard_map/all_gather | solution.py:20
  290.3 7.3 %copy.46 = bf16[4,320,1280]{2,1,0:T(8,128)(2,1)S(1)} copy(bf16[4,320,1280]{1,0,2:T(4,128)(2,1)} %all-gather.9.cloned.1.call-done) | data formatting | bytes 6553600 | tf_op jit(solution)/shard_map/all_gather | solution.py:20
  297.6 28.3 %reduce-scatter.3.cloned.1.call-done = bf16[1024,320]{0,1:T(8,128)(2,1)} async-done(((bf16[1024,1280]{0,1:T(8,128)(2,1)}), bf16[1024,320]{0,1:T(8,128)(2,1)}) %reduce-scatter.3.cloned.1.call-update) | async-done | bytes 655376 | tf_op jit(solution)/shard_map/reduce_scatter | solution.py:25
  326.0 2.4 add_convert_fusion
  328.4 2.2 copy.45
  330.6 2.5 reshape.287
  333.1 3.3 convolution_convert_fusion.1
  336.5 1.2 copy.48
  337.9 0.6 reduce-window.16
  338.5 0.2 slice_reduce_fusion
  338.9 20.6 %reduce-scatter.5.cloned.1.call-done = bf16[256,320]{0,1:T(8,128)(2,1)} async-done(((bf16[256,1280]{0,1:T(8,128)(2,1)}), bf16[256,320]{0,1:T(8,128)(2,1)}) %reduce-scatter.5.cloned.1.call-update) | async-done | bytes 163856 | tf_op jit(solution)/shard_map/reduce_scatter | solution.py:57
  359.5 1.0 add_convert_fusion.1
  360.7 0.8 broadcast_in_dim.47
  361.5 30.6 %scatter_fusion = bf16[64,8,320]{2,1,0:T(8,128)(2,1)} fusion(bf16[64,8,320]{2,1,0:T(8,128)(2,1)} %broadcast_in_dim.47, s32[256]{0:T(256)S(1)} %bitcast.42, bf16[256,320]{1,0:T(8,128)(2,1)S(1)} %copy.47), kind=kCustom, calls=%fused_computation | custom fusion | bytes 493568 | tf_op jit(solution)/shard_map/scatter | solution.py:64
  392.1 12.2 %all-to-all-start = ((bf16[64,8,320]{2,1,0:T(8,128)(2,1)}), bf16[64,8,320]{2,1,0:T(8,128)(2,1)S(1)}, u32[]{:S(2)}, u32[]{:S(2)}) async-start(bf16[64,8,320]{2,1,0:T(8,128)(2,1)} %scatter_fusion), calls=%async_computation.2 | async-start | bytes 786432 | tf_op jit(solution)/shard_map/all_to_all | solution.py:63
  404.6 60.3 %scatter_custom_fusion.2 = s32[512]{0:T(512)S(1)} fusion(s32[16384]{0:T(1024)S(1)} %bitcast.45, s32[16384]{0:T(1024)S(1)} %bitcast.46, s32[]{:T(128)} %constant.43.clone.1), kind=kCustom, calls=%fused_computation.95 | custom fusion | bytes 2052
  465.2 2.6 scatter_custom_fusion.1
  467.7 0.9 copy.49
  (57 shorter events, 1.8 us)
Async XLA Ops:
  6.5 44.2 %all-gather.7.cloned.1.call-start = ((), (), s32[]{:S(2)}) async-start(), calls=%async_computation.3 | async-start | bytes 3276800 | tf_op jit(solution)/shard_map/all_gather | solution.py:10
  7.3 125.7 %all-gather.13.cloned.1.call-start = ((), (), s32[]{:S(2)}) async-start(), calls=%async_computation.8 | async-start | bytes 3993600 | tf_op jit(solution)/shard_map/all_gather | solution.py:19
  8.0 203.7 %all-gather.11.cloned.1.call-start = ((), (), s32[]{:S(2)}) async-start(), calls=%async_computation.7 | async-start | bytes 3993600 | tf_op jit(solution)/shard_map/all_gather | solution.py:18
  8.7 281.6 %all-gather.9.cloned.1.call-start = ((), (), s32[]{:S(2)}) async-start(), calls=%async_computation.5 | async-start | bytes 3993600 | tf_op jit(solution)/shard_map/all_gather | solution.py:20
  9.3 316.6 %reduce-scatter.3.cloned.1.call-start = ((), (), s32[]{:S(2)}) async-start(), calls=%async_computation.4 | async-start | bytes 3276800 | tf_op jit(solution)/shard_map/reduce_scatter | solution.py:25
  50.7 2.5 copy-start
  139.1 78.8 %copy-start.6 = (f32[1280]{0:T(1024)S(1)}, f32[1280]{0:T(1024)}, u32[]{:S(2)}) copy-start(f32[1280]{0:T(1024)} %param.15) | copy-start | bytes 15364
  139.1 78.8 %copy-start.7 = (f32[1280]{0:T(1024)S(1)}, f32[1280]{0:T(1024)}, u32[]{:S(2)}) copy-start(f32[1280]{0:T(1024)} %param.13) | copy-start | bytes 15364
  139.1 78.8 %copy-start.8 = (f32[1280]{0:T(1024)S(1)}, f32[1280]{0:T(1024)}, u32[]{:S(2)}) copy-start(f32[1280]{0:T(1024)} %param.12) | copy-start | bytes 15364
  217.8 21.5 %copy-start.1 = (s32[16384]{0:T(1024)S(1)}, s32[16384]{0:T(1024)}, u32[]{:S(2)}) copy-start(s32[16384]{0:T(1024)} %param.21) | copy-start | bytes 196612
  239.2 86.7 %copy-start.2 = (f32[320]{0:T(512)S(1)}, f32[320]{0:T(512)}, u32[]{:S(2)}) copy-start(f32[320]{0:T(512)} %param.17) | copy-start | bytes 3844
  239.3 120.2 %reduce-scatter.5.cloned.1.call-start = ((), (), s32[]{:S(2)}) async-start(), calls=%async_computation.6 | async-start | bytes 819200 | tf_op jit(solution)/shard_map/reduce_scatter | solution.py:57
  333.1 26.4 %copy-start.3 = (f32[320]{0:T(512)S(1)}, f32[320]{0:T(512)}, u32[]{:S(2)}) copy-start(f32[320]{0:T(512)} %param.19) | copy-start | bytes 3844
  336.4 67.9 %copy-start.5 = (s32[2]{0:T(128)S(1)}, s32[2]{0:T(128)}, u32[]{:S(2)}) copy-start(s32[2]{0:T(128)} %constant.137) | copy-start | bytes 28
  336.4 68.0 %copy-start.4 = (s32[2]{0:T(128)S(1)}, s32[2]{0:T(128)}, u32[]{:S(2)}) copy-start(s32[2]{0:T(128)} %constant.140) | copy-start | bytes 28
  392.1 73.1 %all-to-all-start = ((bf16[64,8,320]{2,1,0:T(8,128)(2,1)}), bf16[64,8,320]{2,1,0:T(8,128)(2,1)S(1)}, u32[]{:S(2)}, u32[]{:S(2)}) async-start(bf16[64,8,320]{2,1,0:T(8,128)(2,1)} %scatter_fusion), calls=%async_computation.2 | async-start | bytes 786432 | tf_op jit(solution)/shard_map/all_to_all | solution.py:63
Sparse Core Ops, SparseCore 0:
  9.2 41.5 all-gather.6
  53.4 79.4 all-gather.12
  135.6 76.0 all-gather.10
  214.3 75.9 all-gather.8
  292.7 33.2 reduce-scatter.2
  336.5 22.9 reduce-scatter.4
where the time goes:
time: 477 us; the launch traced here: 475 us
  waiting for transfers between devices  294 us (62%)
  local copies, waits for them, and re-layouts  122 us (26%)
  matrix products  24.7 us (5%)
  between operations  13.7 us (3%)
  starting transfers between devices  12.4 us (3%)
  other arithmetic  8.4 us (2%)
    all_gather x1, waiting for transfers between devices, per_device(): lax.all_gather(w_out, 'wide', axis=1, tiled=True)  78.9 us
    unnamed x25, local copies, waits for them, and re-layouts  74.1 us
    all_gather x1, waiting for transfers between devices, per_device(): lax.all_gather(w_in, 'wide', axis=0, tiled=True)  72.6 us
    all_gather x1, waiting for transfers between devices, per_device(): lax.all_gather(w_proj, 'wide', axis=2, tiled=True)  49.9 us
    all_gather x1, waiting for transfers between devices, per_device(): whole = lax.all_gather(patches, 'narrow', axis=1, tiled=True)  41.4 us
    scatter x1, local copies, waits for them, and re-layouts, per_device(): buffer.at[own_owners, slot_out].set(vision, mode='drop')  30.6 us
    reduce_scatter x1, waiting for transfers between devices, per_device(): lax.psum_scatter(partial_out.astype(jnp.bfloat16), 'narrow', scatter_dime...  28.3 us
    dot_general x1, matrix products, per_device(): partial_out = jnp.dot(hidden, cols_out, preferred_element_type=jnp.float32)  21.4 us
  transfers between devices with their start and end apart: 7, of which 6 were waited for; matrix products, arithmetic and copies ran while one was open for 23% of the time, Pallas kernels for 0%

commit v1 on v0

v1 whole, which is shorter than its diff:
```python
import jax
import jax.numpy as jnp
from jax import lax
from jax.sharding import PartitionSpec as P


def select_rows(index, rows, count):
    pick = (jnp.arange(count, dtype=jnp.int32)[:, None] == index[None, :]).astype(rows.dtype)
    return jnp.dot(pick, rows, preferred_element_type=jnp.float32).astype(rows.dtype)


def per_device(
    patches, norm_gain, norm_bias, w_in, b_in, w_out, b_out, w_proj, b_proj, text, place
):
    groups = lax.axis_size("wide")
    width = w_in.shape[0]
    local = jnp.concatenate(
        [w_in, w_out.T, w_proj.transpose(2, 0, 1).reshape(width, -1)], axis=0
    )
    gathered = lax.all_gather(local, "wide", axis=0, tiled=False)
    rows_in = gathered[:, :width].reshape(groups * width, -1)
    cols_out = gathered[:, width : 2 * width].reshape(groups * width, -1)
    proj_cols = gathered[:, 2 * width :].reshape(groups * width, -1)

    whole = lax.all_gather(patches, "narrow", axis=1, tiled=True)
    values = whole.astype(jnp.float32)
    center = jnp.mean(values, axis=-1, keepdims=True)
    spread = jnp.mean(jnp.square(values - center), axis=-1, keepdims=True)
    normed = ((values - center) * lax.rsqrt(spread + 1e-06) * norm_gain + norm_bias).astype(
        jnp.bfloat16
    )
    product = jnp.dot(normed, rows_in, preferred_element_type=jnp.float32)
    hidden = jax.nn.gelu(product + b_in, approximate=False).astype(jnp.bfloat16)
    partial_out = lax.dot_general(
        hidden, cols_out, (((1,), (1,)), ((), ())), preferred_element_type=jnp.float32
    )
    mlp_out = lax.psum_scatter(
        partial_out.astype(jnp.bfloat16), "narrow", scatter_dimension=1, tiled=True
    ).astype(jnp.float32)
    stream = (patches.astype(jnp.float32) + (mlp_out + b_out)).astype(jnp.bfloat16)
    merge_count = stream.shape[0] // 4
    merged = stream.reshape(merge_count, 4 * stream.shape[1])
    own_index = lax.axis_index("wide")
    seq_rows = text.shape[0]
    bucket = seq_rows // groups
    place_table = place.reshape(groups, merge_count)
    owners = jnp.where(place_table >= 0, place_table // seq_rows, groups)
    own_owners = lax.dynamic_index_in_dim(owners, own_index, 0, keepdims=False)
    owner_hits = (own_owners[:, None] == jnp.arange(groups, dtype=jnp.int32)[None, :]).astype(
        jnp.int32
    )
    slot_out = jnp.sum(jnp.cumsum(owner_hits, axis=0) * owner_hits, axis=1) - 1
    send_row = jnp.where(
        (own_owners < groups) & (slot_out < bucket), own_owners * bucket + slot_out, -1
    )
    arriving = owners == own_index
    slot_in = jnp.cumsum(arriving.astype(jnp.int32), axis=1) - 1
    slot_in = jnp.where(arriving, slot_in, bucket)
    local_row = place_table % seq_rows
    slot_hits = slot_in[:, :, None] == jnp.arange(bucket, dtype=jnp.int32)[None, None, :]
    targets = jnp.sum(jnp.where(slot_hits, local_row[:, :, None] + 1, 0), axis=1) - 1
    partial_proj = lax.dot_general(
        merged, proj_cols, (((1,), (1,)), ((), ())), preferred_element_type=jnp.float32
    )
    vision = (
        lax.psum_scatter(
            partial_proj.astype(jnp.bfloat16), "narrow", scatter_dimension=1, tiled=True
        ).astype(jnp.float32)
        + b_proj
    ).astype(jnp.bfloat16)
    outgoing = select_rows(send_row, vision, groups * bucket).reshape(groups, bucket, -1)
    received = lax.all_to_all(outgoing, "wide", split_axis=0, concat_axis=0, tiled=True)
    flat_targets = targets.reshape(-1)
    placed = select_rows(flat_targets, received.reshape(-1, received.shape[2]), seq_rows)
    hit = jnp.any(
        jnp.arange(seq_rows, dtype=jnp.int32)[:, None] == flat_targets[None, :], axis=1
    )
    return jnp.where(hit[:, None], placed, text)


def solution(mesh):
    placed = (
        P("wide", "narrow"),
        P(),
        P(),
        P("wide", "narrow"),
        P("narrow"),
        P("narrow", "wide"),
        P("narrow"),
        P(None, "narrow", "wide"),
        P("narrow"),
        P("wide", "narrow"),
        P(),
    )
    return jax.shard_map(
        per_device, mesh=mesh, in_specs=placed, out_specs=P("wide", "narrow"), check_vma=False
    )
```

time: 477 us -> 287 us (0.60)
  waiting for transfers between devices: 294 us -> 189 us
  local copies, waits for them, and re-layouts: 122 us -> 33.5 us
    all_gather x3 -> x1, waiting for transfers between devices: 202 us -> 85.1 us  [per_device(): gathered = lax.all_gather(local, 'wide', axis=0, tiled=False)]
    unnamed x25 -> x15, local copies, waits for them, and re-layouts: 74.1 us -> 1.11 us
    scatter x4 -> x0, local copies, waits for them, and re-layouts: 34.2 us -> none  [the longest x1 30.6 us: per_device(): buffer.at[own_owners, slot_out].set(vision, mode='drop')]
    reduce_scatter x1 -> x0, waiting for transfers between devices: 20.6 us -> none  [per_device(): lax.psum_scatter(partial_proj.astype(jnp.bfloat16), 'narrow', scatter_dim...]
    unnamed x6 -> x5, waiting for transfers between devices: 2.64 us -> 22.5 us
    reshape x1 -> x4, local copies, waits for them, and re-layouts: 0.09 us -> 18 us  [the longest x1 6.28 us: per_device(): rows_in = gathered[:, :width].reshape(groups * width, -1)]
    all_to_all x1, waiting for transfers between devices: 0.01 us -> 13.2 us  [per_device(): lax.all_to_all(outgoing, 'wide', split_axis=0, concat_axis=0, tiled=True)]
    slice x1 -> x2, local copies, waits for them, and re-layouts: 0.18 us -> 8.42 us  [the longest x1 8.25 us: per_device(): proj_cols = gathered[:, 2 * width:].reshape(groups * width, -1)]
  transfers between devices with their start and end apart: 7 -> 5, of which waited for: 6 -> 5; matrix products, arithmetic and copies ran while one was open for 23% -> 5% of each run, Pallas kernels for 0% -> 0%
where the time goes in v1:
time: 287 us
  waiting for transfers between devices  189 us (66%)
  local copies, waits for them, and re-layouts  33.5 us (12%)
  matrix products  26.9 us (9%)
  between operations  13.3 us (5%)
  starting transfers between devices  12 us (4%)
  other arithmetic  11.6 us (4%)
    all_gather x1, waiting for transfers between devices, per_device(): gathered = lax.all_gather(local, 'wide', axis=0, tiled=False)  85.1 us
    all_gather x1, waiting for transfers between devices, per_device(): whole = lax.all_gather(patches, 'narrow', axis=1, tiled=True)  40.8 us
    reduce_scatter x1, waiting for transfers between devices, per_device(): lax.psum_scatter(partial_out.astype(jnp.bfloat16), 'narrow', scatter_dime...  27.8 us
    unnamed x5, waiting for transfers between devices  22.5 us
    dot_general x1, matrix products, per_device(): lax.dot_general(hidden, cols_out, (((1,), (1,)), ((), ())), preferred_ele...  21.5 us
    all_to_all x1, waiting for transfers between devices, per_device(): lax.all_to_all(outgoing, 'wide', split_axis=0, concat_axis=0, tiled=True)  13.2 us
    all_to_all x1, starting transfers between devices, per_device(): lax.all_to_all(outgoing, 'wide', split_axis=0, concat_axis=0, tiled=True)  11.8 us
    slice x1, local copies, waits for them, and re-layouts, per_device(): proj_cols = gathered[:, 2 * width:].reshape(groups * width, -1)  8.25 us
  transfers between devices with their start and end apart: 5, of which 5 were waited for; matrix products, arithmetic and copies ran while one was open for 5% of the time, Pallas kernels for 0%

profile of v1, /device:TPU:1, one launch (start us, length us, event | category | flops | bytes accessed | tf_op | source)
XLA Modules:
  0.0 286.6 jit_solution(14069685264983872683)
XLA Ops:
  6.5 0.7 all-gather.5.cloned.1.call-update
  7.3 0.9 reshape.177
  8.2 1.6 maximum_bitcast_fusion
  9.9 40.8 %all-gather.5.cloned.1.call-done = bf16[1024,1280]{0,1:T(8,128)(2,1)} async-done(((bf16[1024,320]{0,1:T(8,128)(2,1)}), bf16[1024,1280]{0,1:T(8,128)(2,1)}) %all-gather.5.cloned.1.call-update) | async-done | bytes 2621456 | tf_op jit(solution)/shard_map/all_gather | solution.py:25
  50.7 2.2 convert_reduce_fusion
  52.9 2.5 fusion.2
  55.4 85.1 %all-gather.7.cloned.1.call-done = bf16[64,60,1280]{2,1,0:T(8,128)(2,1)} async-done(((bf16[1,60,1280]{2,1,0:T(8,128)(2,1)}), bf16[64,60,1280]{2,1,0:T(8,128)(2,1)}) %all-gather.7.cloned.1.call-update) | async-done | bytes 9830416 | tf_op jit(solution)/shard_map/all_gather | solution.py:20
  140.5 8.2 %fusion.72 = (bf16[64,20,1280]{2,1,0:T(8,128)(2,1)}, bf16[64,20,1280]{2,1,0:T(8,128)(2,1)}, bf16[64,20,1280]{2,1,0:T(8,128)(2,1)}) fusion(bf16[64,60,1280]{2,1,0:T(8,128)(2,1)} %all-gather.7.cloned.1.call-done), kind=kLoop, calls=%fused_computation.116 | loop fusion | bytes 19660800 | tf_op jit(solution)/shard_map/slice | solution.py:23
  148.7 6.1 %reshape.179 = bf16[1280,1280]{1,0:T(8,128)(2,1)} reshape(bf16[64,20,1280]{2,1,0:T(8,128)(2,1)} %get-tuple-element.6) | data formatting | bytes 6553600 | tf_op jit(solution)/shard_map/reshape | solution.py:22
  154.9 6.3 %reshape.178 = bf16[1280,1280]{1,0:T(8,128)(2,1)} reshape(bf16[64,20,1280]{2,1,0:T(8,128)(2,1)} %get-tuple-element.7) | data formatting | bytes 6553600 | tf_op jit(solution)/shard_map/reshape | solution.py:21
  161.2 21.5 %convolution_convert_fusion = bf16[1024,1280]{0,1:T(8,128)(2,1)} fusion(bf16[1280,1280]{1,0:T(8,128)(2,1)} %reshape.179, bf16[1280,1280]{1,0:T(8,128)(2,1)} %reshape.178, bf16[1024,1280]{0,1:T(8,128)(2,1)S(1)} %copy-done, f32[1280]{0:T(1024)S(1)} %copy-done.3, f32[1280]{0:T(1024)S(1)} %copy-done.4, f32[1280]{0:T(1024)S(1)} %copy-done.5, ...), kind=kOutput, calls=%fused_computation.27 | convolution fusion | flops 6806568960 | bytes 11820032 | tf_op jit(solution)/shard_map/dot_general | solution.py:34
  182.9 0.6 reduce-window.14
  183.5 4.6 %reshape.181 = bf16[1280,1280]{1,0:T(8,128)(2,1)S(1)} reshape(bf16[64,20,1280]{2,1,0:T(8,128)(2,1)} %get-tuple-element.5) | data formatting | bytes 6553600 | tf_op jit(solution)/shard_map/reshape | solution.py:23
  188.1 27.8 %reduce-scatter.5.cloned.1.call-done = bf16[1024,320]{0,1:T(8,128)(2,1)} async-done(((bf16[1024,1280]{0,1:T(8,128)(2,1)}), bf16[1024,320]{0,1:T(8,128)(2,1)}) %reduce-scatter.5.cloned.1.call-update) | async-done | bytes 655376 | tf_op jit(solution)/shard_map/reduce_scatter | solution.py:37
  215.9 2.4 add_convert_fusion
  218.3 2.2 copy.38
  220.5 2.5 reshape.180
  223.0 3.0 %fusion.21 = bf16[1280,256]{1,0:T(8,128)(2,1)} fusion(bf16[256,1280]{1,0:T(8,128)(2,1)} %reshape.180, bf16[1280,1280]{1,0:T(8,128)(2,1)S(1)} %reshape.181), kind=kOutput, calls=%fused_computation.33 | convolution fusion | flops 839188480 | bytes 4587520 | tf_op jit(solution)/shard_map/dot_general | solution.py:62
  226.0 0.2 slice_reduce_fusion.1
  226.3 0.1 fusion.30
  226.4 0.6 reduce-window.16
  227.0 0.2 slice_reduce_fusion
  227.2 0.1 fusion.36
  227.4 21.8 %reduce-scatter.7.cloned.1.call-done = bf16[320,256]{1,0:T(8,128)(2,1)} async-done(((bf16[1280,256]{1,0:T(8,128)(2,1)}), bf16[320,256]{1,0:T(8,128)(2,1)}) %reduce-scatter.7.cloned.1.call-update) | async-done | bytes 163856
  249.1 1.1 copy.42
  250.2 0.3 convolution_convert_fusion.2
  250.6 0.9 copy.40
  251.5 11.8 %all-to-all-start = ((bf16[64,8,320]{2,1,0:T(8,128)(2,1)}), bf16[64,8,320]{2,1,0:T(8,128)(2,1)S(1)}, u32[]{:S(2)}, u32[]{:S(2)}) async-start(bf16[64,8,320]{2,1,0:T(8,128)(2,1)} %bitcast.9), calls=%async_computation.1 | async-start | bytes 786432 | tf_op jit(solution)/shard_map/all_to_all | solution.py:72
  263.3 1.2 select_reduce_fusion
  264.6 0.2 fusion.25
  264.8 13.2 %all-to-all-done = bf16[64,8,320]{2,1,0:T(8,128)(2,1)S(1)} async-done(((bf16[64,8,320]{2,1,0:T(8,128)(2,1)}), bf16[64,8,320]{2,1,0:T(8,128)(2,1)S(1)}, u32[]{:S(2)}, u32[]{:S(2)}) %all-to-all-start) | async-done | bytes 327712 | tf_op jit(solution)/shard_map/all_to_all | solution.py:72
  277.9 2.1 fusion.24
  (35 shorter events, 0.5 us)
Async XLA Ops:
  6.5 44.2 %all-gather.5.cloned.1.call-start = ((), (), s32[]{:S(2)}) async-start(), calls=%async_computation.3 | async-start | bytes 3276800 | tf_op jit(solution)/shard_map/all_gather | solution.py:25
  7.3 133.2 %all-gather.7.cloned.1.call-start = ((), (), s32[]{:S(2)}) async-start(), calls=%async_computation.5 | async-start | bytes 10649600 | tf_op jit(solution)/shard_map/all_gather | solution.py:20
  9.8 206.1 %reduce-scatter.5.cloned.1.call-start = ((), (), s32[]{:S(2)}) async-start(), calls=%async_computation.4 | async-start | bytes 3276800 | tf_op jit(solution)/shard_map/reduce_scatter | solution.py:37
  154.9 6.3 %copy-start = (bf16[1024,1280]{0,1:T(8,128)(2,1)S(1)}, bf16[1024,1280]{0,1:T(8,128)(2,1)}, u32[]{:S(2)}) copy-start(bf16[1024,1280]{0,1:T(8,128)(2,1)} %all-gather.5.cloned.1.call-done) | copy-start | bytes 7864324
  154.9 6.3 %copy-start.3 = (f32[1280]{0:T(1024)S(1)}, f32[1280]{0:T(1024)}, u32[]{:S(2)}) copy-start(f32[1280]{0:T(1024)} %param.15) | copy-start | bytes 15364
  154.9 6.3 %copy-start.4 = (f32[1280]{0:T(1024)S(1)}, f32[1280]{0:T(1024)}, u32[]{:S(2)}) copy-start(f32[1280]{0:T(1024)} %param.13) | copy-start | bytes 15364
  154.9 6.3 %copy-start.5 = (f32[1280]{0:T(1024)S(1)}, f32[1280]{0:T(1024)}, u32[]{:S(2)}) copy-start(f32[1280]{0:T(1024)} %param.12) | copy-start | bytes 15364
  161.2 21.6 %copy-start.1 = (s32[16384]{0:T(1024)S(1)}, s32[16384]{0:T(1024)}, u32[]{:S(2)}) copy-start(s32[16384]{0:T(1024)} %param.21) | copy-start | bytes 196612
  182.7 33.2 %copy-start.2 = (f32[320]{0:T(512)S(1)}, f32[320]{0:T(512)}, u32[]{:S(2)}) copy-start(f32[320]{0:T(512)} %param.17) | copy-start | bytes 3844
  182.7 66.4 %reduce-scatter.7.cloned.1.call-start = ((), (), s32[]{:S(2)}) async-start(), calls=%async_computation.6 | async-start | bytes 819200
  218.3 31.9 %copy-start.6 = (f32[320]{0:T(512)S(1)}, f32[320]{0:T(512)}, u32[]{:S(2)}) copy-start(f32[320]{0:T(512)} %param.19) | copy-start | bytes 3844
  251.5 26.4 %all-to-all-start = ((bf16[64,8,320]{2,1,0:T(8,128)(2,1)}), bf16[64,8,320]{2,1,0:T(8,128)(2,1)S(1)}, u32[]{:S(2)}, u32[]{:S(2)}) async-start(bf16[64,8,320]{2,1,0:T(8,128)(2,1)} %bitcast.9), calls=%async_computation.1 | async-start | bytes 786432 | tf_op jit(solution)/shard_map/all_to_all | solution.py:72
Sparse Core Ops, SparseCore 0:
  9.2 41.5 all-gather.4
  53.5 86.9 all-gather.6
  182.8 33.0 reduce-scatter.4
  226.2 22.9 reduce-scatter.6
